TPU v7x, 256 devices: a whole 4x4x8 slice. The times are simulated.
256 devices in a mesh: dp: 32 (over z, y_lo, core), grp: 8 (over y_hi, x).
Axes of the slice: x: 4, y: 4 (y_hi: 2, y_lo: 2; y = y_hi * 2 + y_lo), z: 8, core: 2. Of those that a mesh axis runs over, the one named last changes fastest.
Arguments:
- activations: bfloat16 [16384, 3072], P('dp', 'grp'), may hold values from -125 to 125
- cotangents: bfloat16 [16384, 3072], P('dp', 'grp'), may hold values from -125 to 125
Outputs:
- update: float32 [3072, 3072], P('dp', 'grp')
All inputs are finite; a program needn't handle non-finite values.
Results may differ from a plain program's by a relative error of at most 0.009.
Values may be sent and summed in bfloat16 or wider, within the bound.
No kernel may reach another device: no remote copies, remote signals or barrier semaphores. Data moves between devices by JAX's collectives and lax.ppermute only.
A program may use at most 128 MiB of HBM per device.

v0:
```python
import jax
import jax.numpy as jnp
from jax import lax
from jax.sharding import Mesh
from jax.sharding import PartitionSpec as P

D = 3072
ITERS = 3
GRP = ("grp_0", "grp_1")
DP = ("dp_0", "dp_1", "dp_2")
DP_GRP = ("dp_0", "dp_1", "dp_2", "grp_0", "grp_1")
damping = 0.05
epsilon = 1e-06


def copy_for_each(shard, axis):
    copies = jnp.broadcast_to(shard, (lax.axis_size(axis), *shard.shape))
    return lax.all_to_all(copies, axis, split_axis=0, concat_axis=0, tiled=True)


def in_order(tiles, dim):
    lengths = list(tiles.shape[1:])
    lengths[dim] *= tiles.shape[0]
    return jnp.moveaxis(tiles, 0, dim).reshape(lengths)


def gather_directly(shard, axis, dim):
    tiles = copy_for_each(shard, axis)
    return in_order(tiles, dim)


def sent_together(arrays, axis, dim, along):
    both = jnp.concatenate(arrays, axis=along)
    whole, at, outs = (lax.all_gather(both, axis, axis=dim, tiled=True), 0, [])
    for a in arrays:
        outs.append(lax.slice_in_dim(whole, at, at + a.shape[along], axis=along))
        at += a.shape[along]
    return tuple(outs)


def own_block(tiles, axes, turns):
    inside = tiles.shape[1:]
    tiles = tiles.reshape(*(lax.axis_size(a) for a in axes), *inside)
    tiles = jnp.moveaxis(tiles, turns, range(len(axes))).reshape(-1, *inside)
    for k in turns:
        tiles = lax.psum_scatter(tiles, axes[k], scatter_dimension=0, tiled=True)
    return tiles[0]


def split_up(shard, dim, count):
    before, after = (shard.shape[:dim], shard.shape[dim + 1 :])
    return jnp.moveaxis(shard.reshape(*before, count, -1, *after), dim, 0)


def summed_rows(shard, axes, turns, dim):
    count = lax.axis_size(axes)
    return own_block(split_up(shard, dim, count), axes, turns)


def over_axes(shard, axes):
    for axis in axes:
        shard = lax.psum(shard, axis)
    return shard


def row_panel(stacked_tiles):
    return gather_directly(stacked_tiles, GRP, 2)


def times_columns(panel_rows, stacked_tiles):
    return jnp.einsum(
        "fri,fic->frc",
        panel_rows,
        lax.all_gather(stacked_tiles, DP, axis=1, tiled=True),
        preferred_element_type=jnp.float32,
    )


def shards(activations, cotangents):
    dp_count = lax.axis_size(DP)
    grp_count = lax.axis_size(GRP)
    tile_rows = D // dp_count
    tile_cols = D // grp_count
    dp_index = lax.axis_index(DP)
    grp_index = lax.axis_index(GRP)
    whole_inputs, whole_grads = sent_together((activations, cotangents), GRP, 1, 0)
    contract = (((0,), (0,)), ((), ()))
    row_ids = dp_index * tile_rows + lax.iota(jnp.int32, tile_rows)[:, None]
    col_ids = grp_index * tile_cols + lax.iota(jnp.int32, tile_cols)[None, :]
    diag_tile = (row_ids == col_ids).astype(jnp.float32)
    diag_rows = (row_ids == lax.iota(jnp.int32, D)[None, :]).astype(jnp.float32)
    gradient_tile = None
    grads_part = whole_grads
    input_cov = lax.dot_general(
        whole_inputs, activations, contract, preferred_element_type=jnp.float32
    )
    grad_cov = lax.dot_general(grads_part, cotangents, contract, preferred_element_type=jnp.float32)
    input_cov, grad_cov = (input_cov, grad_cov)
    grads_part = whole_grads
    weight_grad = lax.dot_general(
        grads_part, activations, contract, preferred_element_type=jnp.float32
    )
    sum_tiles = summed_rows(
        jnp.concatenate([input_cov, grad_cov, weight_grad], axis=1), DP, (2, 0, 1), 0
    )
    gradient_tile = sum_tiles[:, 2 * tile_cols :]
    factor_tiles = jnp.stack([sum_tiles[:, :tile_cols], sum_tiles[:, tile_cols : 2 * tile_cols]])
    trace_parts = jnp.sum(factor_tiles * diag_tile[None], axis=(1, 2))
    square_parts = jnp.sum(factor_tiles * factor_tiles, axis=(1, 2))
    trace_sums, square_sums = (over_axes(trace_parts, DP_GRP), over_axes(square_parts, DP_GRP))
    damp_terms = damping * trace_sums / D
    norm_square = square_sums + 2.0 * damp_terms * trace_sums + D * damp_terms * damp_terms
    scale_factors = lax.rsqrt(norm_square)[:, None, None]
    base_tiles = (
        scale_factors * (factor_tiles + damp_terms[:, None, None] * diag_tile[None])
    ).astype(jnp.bfloat16)
    base_rows = row_panel(base_tiles)
    iterate_tiles = (2.0 * diag_tile[None] - base_tiles.astype(jnp.float32)).astype(jnp.bfloat16)
    iterate_rows = (2.0 * diag_rows[None] - base_rows.astype(jnp.float32)).astype(jnp.bfloat16)
    for sweep_index in range(ITERS - 1):
        product = times_columns(base_rows, iterate_tiles)
        product_tiles = product.astype(jnp.bfloat16)
        updated = 2.0 * iterate_tiles.astype(jnp.float32) - times_columns(
            iterate_rows, product_tiles
        )
        iterate_tiles = updated.astype(jnp.bfloat16)
        if sweep_index + 2 < ITERS:
            iterate_rows = row_panel(iterate_tiles)
    inverse_rows = row_panel(iterate_tiles[1:2])
    left_side = times_columns(inverse_rows, gradient_tile.astype(jnp.bfloat16)[None])
    left_tiles = left_side.astype(jnp.bfloat16)
    left_rows = row_panel(left_tiles)
    preconditioned = times_columns(left_rows, iterate_tiles[0:1])[0]
    square_total = over_axes(jnp.sum(preconditioned * preconditioned), DP_GRP)
    return preconditioned * lax.rsqrt(square_total / (D * D) + epsilon)


def solution(mesh):
    split = Mesh(mesh.devices.reshape(8, 2, 2, 2, 4), ("dp_0", "dp_1", "dp_2", "grp_0", "grp_1"))
    return jax.shard_map(
        shards, mesh=split, in_specs=(P(DP, GRP), P(DP, GRP)), out_specs=P(DP, GRP), check_vma=False
    )
```

profile of v0, /device:TPU:16, one launch (start us, length us, event | category | flops | bytes accessed | tf_op | source)
XLA Modules:
  0.0 806.2 jit_solution(5513607981691237652)
XLA Ops:
  8.7 104.8 %all-gather.9.cloned.1.call-done = bf16[1024,3072]{1,0:T(8,128)(2,1)} async-done(((bf16[1024,384]{1,0:T(8,128)(2,1)}), bf16[1024,3072]{1,0:T(8,128)(2,1)}) %all-gather.9.cloned.1.call-update) | async-done | bytes 6291472 | tf_op jit(solution)/shard_map/all_gather | solution.py:34
  120.3 5.7 pad_maximum_fusion
  126.0 15.2 %copy.6 = f32[3072,1152]{1,0:T(8,128)} copy(f32[3072,1152]{0,1:T(8,128)} %pad_maximum_fusion) | data formatting | bytes 28311552 | tf_op jit(solution)/shard_map/concatenate | solution.py:104
  141.2 11.4 %copy.7 = f32[2,8,2,96,1152]{4,3,2,1,0:T(8,128)} copy(f32[2,8,2,96,1152]{4,3,0,2,1:T(8,128)} %bitcast.48) | data formatting | bytes 28311552 | tf_op jit(solution)/shard_map/transpose | solution.py:44
  152.6 31.1 %reduce-scatter.4.cloned.1.call-done = f32[16,96,1152]{2,1,0:T(8,128)} async-done(((f32[32,96,1152]{2,1,0:T(8,128)}), f32[16,96,1152]{2,1,0:T(8,128)}) %reduce-scatter.4.cloned.1.call-update) | async-done | bytes 7077904 | tf_op jit(solution)/shard_map/reduce_scatter | solution.py:46
  183.8 86.4 %reduce-scatter.6.cloned.1.call-done = f32[2,96,1152]{2,1,0:T(8,128)} async-done(((f32[16,96,1152]{2,1,0:T(8,128)}), f32[2,96,1152]{2,1,0:T(8,128)}) %reduce-scatter.6.cloned.1.call-update) | async-done | bytes 884752 | tf_op jit(solution)/shard_map/reduce_scatter | solution.py:46
  270.4 24.2 %reduce-scatter.8.cloned.1.call-done = f32[1,96,1152]{2,1,0:T(8,128)} async-done(((f32[2,96,1152]{2,1,0:T(8,128)}), f32[1,96,1152]{2,1,0:T(8,128)}) %reduce-scatter.8.cloned.1.call-update) | async-done | bytes 442384 | tf_op jit(solution)/shard_map/reduce_scatter | solution.py:46
  295.8 17.5 %all-reduce = (f32[2]{0:T(128)S(1)}, f32[2]{0:T(128)S(1)}) all-reduce(f32[2]{0:T(128)S(1)} %get-tuple-element.6, f32[2]{0:T(128)S(1)} %get-tuple-element.5), channel_id=1, replica_groups=mesh['dp_0'=8,'dp_1'=2,'dp_2'=2,'grp_0'=2,'grp_1'=4] {'dp_0'}, use_global_device_ids=true, to_apply=%region_10.0 | all-reduce | flops 4 | bytes 32 | tf_op jit(solution)/shard_map/psum | solution.py:62
  320.6 6.4 all-reduce.2
  327.0 10.4 %all-reduce.1 = (f32[2]{0:T(128)S(1)}, f32[2]{0:T(128)S(1)}) all-reduce(f32[2]{0:T(128)S(1)} %get-tuple-element.11, f32[2]{0:T(128)S(1)} %get-tuple-element.12), channel_id=1, replica_groups=mesh['dp_0'=8,'dp_1'=2,'dp_2'=2,'grp_0'=2,'grp_1'=4] {'grp_1'}, use_global_device_ids=true, to_apply=%region_14.0 | all-reduce | flops 4 | bytes 32 | tf_op jit(solution)/shard_map/psum | solution.py:62
  338.4 17.9 %all_to_all.20 = bf16[8,2,96,384]{3,2,1,0:T(8,128)(2,1)S(1)} all-to-all(bf16[8,2,96,384]{3,2,1,0:T(8,128)(2,1)S(1)} %broadcast_in_dim.10), channel_id=1, replica_groups=mesh['dp_0'=8,'dp_1'=2,'dp_2'=2,'grp_0'=2,'grp_1'=4] {'grp_0','grp_1'}, dimensions={0} | all-to-all | bytes 2359296 | tf_op jit(solution)/shard_map/all_to_all | solution.py:18
  356.5 47.5 %all-gather.11.cloned.1.call-done = bf16[2,3072,384]{2,1,0:T(8,128)(2,1)} async-done(((bf16[2,96,384]{2,1,0:T(8,128)(2,1)}), bf16[2,3072,384]{2,1,0:T(8,128)(2,1)}) %all-gather.11.cloned.1.call-update) | async-done | bytes 4718608 | tf_op jit(solution)/shard_map/all_gather | solution.py:74
  408.2 65.1 %all-gather.13.cloned.1.call-done = bf16[2,3072,384]{2,1,0:T(8,128)(2,1)} async-done(((bf16[2,96,384]{2,1,0:T(8,128)(2,1)}), bf16[2,3072,384]{2,1,0:T(8,128)(2,1)}) %all-gather.13.cloned.1.call-update) | async-done | bytes 4718608 | tf_op jit(solution)/shard_map/all_gather | solution.py:74
  477.3 67.0 %all-gather.15.cloned.1.call-done = bf16[2,3072,384]{2,1,0:T(8,128)(2,1)} async-done(((bf16[2,96,384]{2,1,0:T(8,128)(2,1)}), bf16[2,3072,384]{2,1,0:T(8,128)(2,1)}) %all-gather.15.cloned.1.call-update) | async-done | bytes 4718608 | tf_op jit(solution)/shard_map/all_gather | solution.py:74
  550.1 23.0 %all_to_all.21 = bf16[8,2,96,384]{3,2,1,0:T(8,128)(2,1)S(1)} all-to-all(bf16[8,2,96,384]{3,2,1,0:T(8,128)(2,1)S(1)} %broadcast_in_dim.11), channel_id=1, replica_groups=mesh['dp_0'=8,'dp_1'=2,'dp_2'=2,'grp_0'=2,'grp_1'=4] {'grp_0','grp_1'}, dimensions={0} | all-to-all | bytes 2359296 | tf_op jit(solution)/shard_map/all_to_all | solution.py:18
  573.3 46.7 %all-gather.17.cloned.1.call-done = bf16[2,3072,384]{2,1,0:T(8,128)(2,1)} async-done(((bf16[2,96,384]{2,1,0:T(8,128)(2,1)}), bf16[2,3072,384]{2,1,0:T(8,128)(2,1)}) %all-gather.17.cloned.1.call-update) | async-done | bytes 4718608 | tf_op jit(solution)/shard_map/all_gather | solution.py:74
  624.1 17.1 %all_to_all.22 = bf16[8,1,96,384]{3,2,1,0:T(8,128)(2,1)S(1)} all-to-all(bf16[8,1,96,384]{3,2,1,0:T(8,128)(2,1)S(1)} %broadcast_in_dim.12), channel_id=1, replica_groups=mesh['dp_0'=8,'dp_1'=2,'dp_2'=2,'grp_0'=2,'grp_1'=4] {'grp_0','grp_1'}, dimensions={0} | all-to-all | bytes 1179648 | tf_op jit(solution)/shard_map/all_to_all | solution.py:18
  641.2 44.7 %all-gather.21.cloned.1.call-done = bf16[3072,384]{1,0:T(8,128)(2,1)} async-done(((bf16[96,384]{1,0:T(8,128)(2,1)}), bf16[3072,384]{1,0:T(8,128)(2,1)}) %all-gather.21.cloned.1.call-update) | async-done | bytes 2359312 | tf_op jit(solution)/shard_map/all_gather | solution.py:74
  688.2 16.8 %all_to_all.23 = bf16[8,1,96,384]{3,2,1,0:T(8,128)(2,1)S(1)} all-to-all(bf16[8,1,96,384]{3,2,1,0:T(8,128)(2,1)S(1)} %broadcast_in_dim.28), channel_id=1, replica_groups=mesh['dp_0'=8,'dp_1'=2,'dp_2'=2,'grp_0'=2,'grp_1'=4] {'grp_0','grp_1'}, dimensions={0} | all-to-all | bytes 1179648 | tf_op jit(solution)/shard_map/all_to_all | solution.py:18
  705.0 46.9 %all-gather.19.cloned.1.call-done = bf16[1,3072,384]{2,1,0:T(8,128)(2,1)} async-done(((bf16[1,96,384]{2,1,0:T(8,128)(2,1)}), bf16[1,3072,384]{2,1,0:T(8,128)(2,1)}) %all-gather.19.cloned.1.call-update) | async-done | bytes 2359312 | tf_op jit(solution)/shard_map/all_gather | solution.py:74
  754.7 16.6 %psum.115 = f32[]{:T(128)} all-reduce(f32[]{:T(128)} %get-tuple-element.25), channel_id=1, replica_groups=mesh['dp_0'=8,'dp_1'=2,'dp_2'=2,'grp_0'=2,'grp_1'=4] {'dp_0'}, use_global_device_ids=true, to_apply=%region_16.0 | all-reduce | flops 1 | bytes 8 | tf_op jit(solution)/shard_map/psum | solution.py:62
  771.3 5.5 psum.116
  779.9 7.1 psum.118
  787.0 11.1 %psum.119 = f32[]{:T(128)} all-reduce(f32[]{:T(128)} %psum.118), channel_id=1, replica_groups=mesh['dp_0'=8,'dp_1'=2,'dp_2'=2,'grp_0'=2,'grp_1'=4] {'grp_1'}, use_global_device_ids=true, to_apply=%region_20.0 | all-reduce | flops 1 | bytes 8 | tf_op jit(solution)/shard_map/psum | solution.py:62
  (63 shorter events, 46.1 us)
Async XLA Ops:
  6.5 106.9 %all-gather.9.cloned.1.call-start = ((), (), s32[]{:S(2)}) async-start(), calls=%async_computation.7 | async-start | bytes 7077888 | tf_op jit(solution)/shard_map/all_gather | solution.py:34
  8.6 108.4 %copy-start.2 = (bf16[512,384]{1,0:T(8,128)(2,1)S(1)}, bf16[512,384]{1,0:T(8,128)(2,1)}, u32[]{:S(2)}) copy-start(bf16[512,384]{1,0:T(8,128)(2,1)} %param.2) | copy-start | bytes 1179652
  8.7 175.1 %reduce-scatter.4.cloned.1.call-start = ((), (), s32[]{:S(2)}) async-start(), calls=%async_computation.8 | async-start | bytes 21233664 | tf_op jit(solution)/shard_map/reduce_scatter | solution.py:46
  113.5 3.8 copy-start
  117.3 1.5 copy-start.3
  152.6 117.6 %reduce-scatter.6.cloned.1.call-start = ((), (), s32[]{:S(2)}) async-start(), calls=%async_computation.9 | async-start | bytes 7962624 | tf_op jit(solution)/shard_map/reduce_scatter | solution.py:46
  183.7 110.8 %reduce-scatter.8.cloned.1.call-start = ((), (), s32[]{:S(2)}) async-start(), calls=%async_computation.10 | async-start | bytes 1327104 | tf_op jit(solution)/shard_map/reduce_scatter | solution.py:46
  270.2 133.8 %all-gather.11.cloned.1.call-start = ((), (), s32[]{:S(2)}) async-start(), calls=%async_computation.11 | async-start | bytes 4866048 | tf_op jit(solution)/shard_map/all_gather | solution.py:74
  338.2 135.1 %all-gather.13.cloned.1.call-start = ((), (), s32[]{:S(2)}) async-start(), calls=%async_computation.12 | async-start | bytes 4866048 | tf_op jit(solution)/shard_map/all_gather | solution.py:74
  404.0 69.3 %copy-start.4 = (bf16[2,96,384]{2,1,0:T(8,128)(2,1)S(1)}, bf16[2,96,384]{2,1,0:T(8,128)(2,1)}, u32[]{:S(2)}) copy-start(bf16[2,96,384]{2,1,0:T(8,128)(2,1)} %get-tuple-element.17) | copy-start | bytes 442372
  407.9 136.4 %all-gather.15.cloned.1.call-start = ((), (), s32[]{:S(2)}) async-start(), calls=%async_computation.13 | async-start | bytes 4866048 | tf_op jit(solution)/shard_map/all_gather | solution.py:74
  477.2 72.7 %copy-start.1 = (bf16[2,96,384]{2,1,0:T(8,128)(2,1)S(1)}, bf16[2,96,384]{2,1,0:T(8,128)(2,1)}, u32[]{:S(2)}) copy-start(bf16[2,96,384]{2,1,0:T(8,128)(2,1)} %fusion.12) | copy-start | bytes 442372
  477.2 142.8 %all-gather.17.cloned.1.call-start = ((), (), s32[]{:S(2)}) async-start(), calls=%async_computation.14 | async-start | bytes 4866048 | tf_op jit(solution)/shard_map/all_gather | solution.py:74
  548.3 137.7 %all-gather.21.cloned.1.call-start = ((), (), s32[]{:S(2)}) async-start(), calls=%async_computation.16 | async-start | bytes 2433024 | tf_op jit(solution)/shard_map/all_gather | solution.py:74
  549.9 202.0 %all-gather.19.cloned.1.call-start = ((), (), s32[]{:S(2)}) async-start(), calls=%async_computation.15 | async-start | bytes 2433024 | tf_op jit(solution)/shard_map/all_gather | solution.py:74
Sparse Core Ops, SparseCore 0:
  9.8 103.6 all-gather.8
  152.7 30.9 reduce-scatter.3
  186.3 83.8 reduce-scatter.5
  272.5 22.0 reduce-scatter.7
  338.3 65.5 all-gather.10
  408.1 65.1 all-gather.12
  477.3 66.9 all-gather.14
  548.4 71.6 all-gather.16
  621.9 63.9 all-gather.20
  687.6 64.2 all-gather.18
where the time goes:
time: 807 us; the launch traced here: 806 us
  waiting for transfers between devices  564 us (70%)
  blocking collectives  160 us (20%)
  local copies, waits for them, and re-layouts  30.9 us (4%)
  matrix products  26.7 us (3%)
  between operations  14.4 us (2%)
  other arithmetic  9.71 us (1%)
    all_gather x6, waiting for transfers between devices, times_columns(): lax.all_gather(stacked_tiles, DP, axis=1, tiled=True)  318 us
    reduce_scatter x3, waiting for transfers between devices, own_block(): tiles = lax.psum_scatter(tiles, axes[k], scatter_dimension=0, tiled=True)  142 us
    all_gather x1, waiting for transfers between devices, sent_together(): whole, at, outs = (lax.all_gather(both, axis, axis=dim, tiled=True), 0, [])  105 us
    psum x10, blocking collectives, over_axes(): shard = lax.psum(shard, axis)  84.9 us
    all_to_all x4, blocking collectives, copy_for_each(): return lax.all_to_all(copies, axis, split_axis=0, concat_axis=0, tiled=True)  74.8 us
    dot_general x6, matrix products, times_columns(): jnp.einsum('fri,fic->frc', panel_rows, lax.all_gather(stacked_tiles, DP,...  20.1 us
  transfers between devices with their start and end apart: 10, of which 10 were waited for; matrix products, arithmetic and copies ran while one was open for 1% of the time, Pallas kernels for 0%

commit v1 on v0

--- a/solution.py
+++ b/solution.py
@@ -11,6 +11,11 @@
 DP_GRP = ("dp_0", "dp_1", "dp_2", "grp_0", "grp_1")
 damping = 0.05
 epsilon = 1e-06
+
+
+def swapped_in(x, axis, dim):
+    sent = jnp.stack([x] * lax.axis_size(axis))
+    return jnp.concatenate(lax.all_to_all(sent, axis, 0, 0), axis=dim)
 
 
 def copy_for_each(shard, axis):
@@ -71,7 +76,7 @@
     return jnp.einsum(
         "fri,fic->frc",
         panel_rows,
-        lax.all_gather(stacked_tiles, DP, axis=1, tiled=True),
+        swapped_in(stacked_tiles, DP, 1),
         preferred_element_type=jnp.float32,
     )
 

time: 807 us -> 1060 us (1.31)
  waiting for transfers between devices: 564 us -> 694 us
  blocking collectives: 160 us -> 230 us
  starting transfers between devices: 0.37 us -> 39.8 us
  local copies, waits for them, and re-layouts: 30.9 us -> 56.9 us
  matrix products: 26.7 us -> 12.3 us
    all_to_all x0 -> x7, waiting for transfers between devices: none -> 447 us  [the longest x5 429 us: swapped_in(): return jnp.concatenate(lax.all_to_all(sent, axis, 0, 0), axis=dim)]
    all_gather x6 -> x0, waiting for transfers between devices: 318 us -> none  [times_columns(): lax.all_gather(stacked_tiles, DP, axis=1, tiled=True)]
    all_to_all x0 -> x1, blocking collectives: none -> 113 us  [swapped_in(): return jnp.concatenate(lax.all_to_all(sent, axis, 0, 0), axis=dim)]
    all_to_all x4 -> x2, blocking collectives: 74.8 us -> 32.8 us  [copy_for_each(): return lax.all_to_all(copies, axis, split_axis=0, concat_axis=0, tiled=True)]
    all_to_all x0 -> x7, starting transfers between devices: none -> 39.6 us  [the longest x5 27 us: swapped_in(): return jnp.concatenate(lax.all_to_all(sent, axis, 0, 0), axis=dim)]
    dot_general x6, matrix products: 20.1 us -> 5.68 us  [times_columns(): jnp.einsum('fri,fic->frc', panel_rows, swapped_in(stacked_tiles, DP, 1),...]
    another operation x0 -> x6, local copies, waits for them, and re-layouts: none -> 13.5 us  [swapped_in(): sent = jnp.stack([x] * lax.axis_size(axis))]
    reshape x0 -> x4, local copies, waits for them, and re-layouts: none -> 11.2 us  [swapped_in(): return jnp.concatenate(lax.all_to_all(sent, axis, 0, 0), axis=dim)]
  transfers between devices with their start and end apart: 10 -> 11, of which waited for: 10 -> 11; matrix products, arithmetic and copies ran while one was open for 1% -> 1% of each run, Pallas kernels for 0% -> 0%
where the time goes in v1:
time: 1060 us
  waiting for transfers between devices  694 us (65%)
  blocking collectives  230 us (22%)
  local copies, waits for them, and re-layouts  56.9 us (5%)
  starting transfers between devices  39.8 us (4%)
  between operations  14.1 us (1%)
  matrix products  12.3 us (1%)
    all_to_all x5, waiting for transfers between devices, swapped_in(): return jnp.concatenate(lax.all_to_all(sent, axis, 0, 0), axis=dim)  429 us
    reduce_scatter x3, waiting for transfers between devices, own_block(): tiles = lax.psum_scatter(tiles, axes[k], scatter_dimension=0, tiled=True)  142 us
    all_to_all x1, blocking collectives, swapped_in(): return jnp.concatenate(lax.all_to_all(sent, axis, 0, 0), axis=dim)  113 us
    all_gather x1, waiting for transfers between devices, sent_together(): whole, at, outs = (lax.all_gather(both, axis, axis=dim, tiled=True), 0, [])  105 us
    psum x10, blocking collectives, over_axes(): shard = lax.psum(shard, axis)  83.9 us
    all_to_all x2, blocking collectives, copy_for_each(): return lax.all_to_all(copies, axis, split_axis=0, concat_axis=0, tiled=True)  32.8 us
    all_to_all x5, starting transfers between devices, swapped_in(): return jnp.concatenate(lax.all_to_all(sent, axis, 0, 0), axis=dim)  27 us
  transfers between devices with their start and end apart: 11, of which 11 were waited for; matrix products, arithmetic and copies ran while one was open for 1% of the time, Pallas kernels for 0%

profile of v1, /device:TPU:16, one launch (start us, length us, event | category | flops | bytes accessed | tf_op | source)
XLA Modules:
  0.0 1055.9 jit_solution(13868586909384710988)
XLA Ops:
  8.7 104.8 %all-gather.2.cloned.1.call-done = bf16[1024,3072]{1,0:T(8,128)(2,1)} async-done(((bf16[1024,384]{1,0:T(8,128)(2,1)}), bf16[1024,3072]{1,0:T(8,128)(2,1)}) %all-gather.2.cloned.1.call-update) | async-done | bytes 6291472 | tf_op jit(solution)/shard_map/all_gather | solution.py:39
  126.0 15.2 %copy.6 = f32[3072,1152]{1,0:T(8,128)} copy(f32[3072,1152]{0,1:T(8,128)} %pad_maximum_fusion) | data formatting | bytes 28311552 | tf_op jit(solution)/shard_map/concatenate | solution.py:109
  141.2 11.4 %copy.7 = f32[2,8,2,96,1152]{4,3,2,1,0:T(8,128)} copy(f32[2,8,2,96,1152]{4,3,0,2,1:T(8,128)} %bitcast.56) | data formatting | bytes 28311552 | tf_op jit(solution)/shard_map/transpose | solution.py:49
  152.6 31.1 %reduce-scatter.4.cloned.1.call-done = f32[16,96,1152]{2,1,0:T(8,128)} async-done(((f32[32,96,1152]{2,1,0:T(8,128)}), f32[16,96,1152]{2,1,0:T(8,128)}) %reduce-scatter.4.cloned.1.call-update) | async-done | bytes 7077904 | tf_op jit(solution)/shard_map/reduce_scatter | solution.py:51
  183.8 86.4 %reduce-scatter.6.cloned.1.call-done = f32[2,96,1152]{2,1,0:T(8,128)} async-done(((f32[16,96,1152]{2,1,0:T(8,128)}), f32[2,96,1152]{2,1,0:T(8,128)}) %reduce-scatter.6.cloned.1.call-update) | async-done | bytes 884752 | tf_op jit(solution)/shard_map/reduce_scatter | solution.py:51
  270.4 24.2 %reduce-scatter.8.cloned.1.call-done = f32[1,96,1152]{2,1,0:T(8,128)} async-done(((f32[2,96,1152]{2,1,0:T(8,128)}), f32[1,96,1152]{2,1,0:T(8,128)}) %reduce-scatter.8.cloned.1.call-update) | async-done | bytes 442384 | tf_op jit(solution)/shard_map/reduce_scatter | solution.py:51
  295.7 17.5 %all-reduce = (f32[2]{0:T(128)S(1)}, f32[2]{0:T(128)S(1)}) all-reduce(f32[2]{0:T(128)S(1)} %get-tuple-element.6, f32[2]{0:T(128)S(1)} %get-tuple-element.5), channel_id=1, replica_groups=mesh['dp_0'=8,'dp_1'=2,'dp_2'=2,'grp_0'=2,'grp_1'=4] {'dp_0'}, use_global_device_ids=true, to_apply=%region_10.0 | all-reduce | flops 4 | bytes 32 | tf_op jit(solution)/shard_map/psum | solution.py:67
  320.6 6.4 all-reduce.2
  327.0 10.4 all-reduce.1
  337.6 17.7 %all_to_all.50 = bf16[8,2,96,384]{3,2,1,0:T(8,128)(2,1)S(1)} all-to-all(bf16[8,2,96,384]{3,2,1,0:T(8,128)(2,1)S(1)} %broadcast_in_dim.8), channel_id=1, replica_groups=mesh['dp_0'=8,'dp_1'=2,'dp_2'=2,'grp_0'=2,'grp_1'=4] {'grp_0','grp_1'}, dimensions={0} | all-to-all | bytes 2359296 | tf_op jit(solution)/shard_map/all_to_all | solution.py:23
  363.6 105.2 %all-to-all-done.1 = bf16[32,2,96,384]{3,2,1,0:T(8,128)(2,1)} async-done(((bf16[32,2,96,384]{3,2,1,0:T(8,128)(2,1)}), bf16[32,2,96,384]{3,2,1,0:T(8,128)(2,1)}, u32[]{:S(2)}, u32[]{:S(2)}) %all-to-all-start.1) | async-done | bytes 4718624 | tf_op jit(solution)/shard_map/all_to_all | solution.py:18
  481.7 104.9 %all-to-all-done.2 = bf16[32,2,96,384]{3,2,1,0:T(8,128)(2,1)} async-done(((bf16[32,2,96,384]{3,2,1,0:T(8,128)(2,1)}), bf16[32,2,96,384]{3,2,1,0:T(8,128)(2,1)}, u32[]{:S(2)}, u32[]{:S(2)}) %all-to-all-start.2) | async-done | bytes 4718624 | tf_op jit(solution)/shard_map/all_to_all | solution.py:18
  591.2 113.2 %all_to_all.51 = bf16[32,2,96,384]{3,2,1,0:T(8,128)(2,1)} all-to-all(bf16[32,2,96,384]{3,2,1,0:T(8,128)(2,1)S(1)} %stack.23), channel_id=1, replica_groups=mesh['dp_0'=8,'dp_1'=2,'dp_2'=2,'grp_0'=2,'grp_1'=4] {'dp_0','dp_1','dp_2'}, dimensions={0} | all-to-all | bytes 9437184 | tf_op jit(solution)/shard_map/all_to_all | solution.py:18
  705.6 6.2 all-to-all-start.3
  715.6 11.7 %all-to-all-done.3 = bf16[8,2,96,384]{3,2,1,0:T(8,128)(2,1)S(1)} async-done(((bf16[8,2,96,384]{3,2,1,0:T(8,128)(2,1)}), bf16[8,2,96,384]{3,2,1,0:T(8,128)(2,1)S(1)}, u32[]{:S(2)}, u32[]{:S(2)}) %all-to-all-start.3) | async-done | bytes 1179680 | tf_op jit(solution)/shard_map/all_to_all | solution.py:23
  735.3 107.6 %all-to-all-done.5 = bf16[32,2,96,384]{3,2,1,0:T(8,128)(2,1)} async-done(((bf16[32,2,96,384]{3,2,1,0:T(8,128)(2,1)}), bf16[32,2,96,384]{3,2,1,0:T(8,128)(2,1)}, u32[]{:S(2)}, u32[]{:S(2)}) %all-to-all-start.5) | async-done | bytes 4718624 | tf_op jit(solution)/shard_map/all_to_all | solution.py:18
  848.2 6.5 all-to-all-start.6
  855.6 6.6 all-to-all-done.6
  870.0 55.7 %all-to-all-done.7 = bf16[32,1,96,384]{3,2,1,0:T(8,128)(2,1)S(1)} async-done(((bf16[32,1,96,384]{3,2,1,0:T(8,128)(2,1)}), bf16[32,1,96,384]{3,2,1,0:T(8,128)(2,1)S(1)}, u32[]{:S(2)}, u32[]{:S(2)}) %all-to-all-start.7) | async-done | bytes 2359328 | tf_op jit(solution)/shard_map/all_to_all | solution.py:18
  926.3 15.1 %all_to_all.52 = bf16[8,1,96,384]{3,2,1,0:T(8,128)(2,1)S(1)} all-to-all(bf16[8,1,96,384]{3,2,1,0:T(8,128)(2,1)S(1)} %broadcast_in_dim.11), channel_id=1, replica_groups=mesh['dp_0'=8,'dp_1'=2,'dp_2'=2,'grp_0'=2,'grp_1'=4] {'grp_0','grp_1'}, dimensions={0} | all-to-all | bytes 1179648 | tf_op jit(solution)/shard_map/all_to_all | solution.py:23
  948.9 55.7 %all-to-all-done.9 = bf16[32,1,96,384]{3,2,1,0:T(8,128)(2,1)S(1)} async-done(((bf16[32,1,96,384]{3,2,1,0:T(8,128)(2,1)}), bf16[32,1,96,384]{3,2,1,0:T(8,128)(2,1)S(1)}, u32[]{:S(2)}, u32[]{:S(2)}) %all-to-all-start.9) | async-done | bytes 2359328 | tf_op jit(solution)/shard_map/all_to_all | solution.py:18
  1005.7 16.9 %psum.115 = f32[]{:T(128)} all-reduce(f32[]{:T(128)} %get-tuple-element.25), channel_id=1, replica_groups=mesh['dp_0'=8,'dp_1'=2,'dp_2'=2,'grp_0'=2,'grp_1'=4] {'dp_0'}, use_global_device_ids=true, to_apply=%region_16.0 | all-reduce | flops 1 | bytes 8 | tf_op jit(solution)/shard_map/psum | solution.py:67
  1031.3 7.1 psum.118
  1038.3 9.7 psum.119
  (64 shorter events, 94.9 us)
Async XLA Ops:
  6.5 106.9 %all-gather.2.cloned.1.call-start = ((), (), s32[]{:S(2)}) async-start(), calls=%async_computation.13 | async-start | bytes 7077888 | tf_op jit(solution)/shard_map/all_gather | solution.py:39
  8.6 108.4 %copy-start.1 = (bf16[512,384]{1,0:T(8,128)(2,1)S(1)}, bf16[512,384]{1,0:T(8,128)(2,1)}, u32[]{:S(2)}) copy-start(bf16[512,384]{1,0:T(8,128)(2,1)} %param.2) | copy-start | bytes 1179652
  8.7 175.1 %reduce-scatter.4.cloned.1.call-start = ((), (), s32[]{:S(2)}) async-start(), calls=%async_computation.14 | async-start | bytes 21233664 | tf_op jit(solution)/shard_map/reduce_scatter | solution.py:51
  113.5 3.8 copy-start
  117.3 1.5 copy-start.2
  152.6 117.6 %reduce-scatter.6.cloned.1.call-start = ((), (), s32[]{:S(2)}) async-start(), calls=%async_computation.15 | async-start | bytes 7962624 | tf_op jit(solution)/shard_map/reduce_scatter | solution.py:51
  183.7 110.8 %reduce-scatter.8.cloned.1.call-start = ((), (), s32[]{:S(2)}) async-start(), calls=%async_computation.16 | async-start | bytes 1327104 | tf_op jit(solution)/shard_map/reduce_scatter | solution.py:51
  358.2 110.5 %all-to-all-start.1 = ((bf16[32,2,96,384]{3,2,1,0:T(8,128)(2,1)}), bf16[32,2,96,384]{3,2,1,0:T(8,128)(2,1)}, u32[]{:S(2)}, u32[]{:S(2)}) async-start(bf16[32,2,96,384]{3,2,1,0:T(8,128)(2,1)} %stack.21), calls=%async_computation.4 | async-start | bytes 9437184 | tf_op jit(solution)/shard_map/all_to_all | solution.py:18
  475.4 111.2 %all-to-all-start.2 = ((bf16[32,2,96,384]{3,2,1,0:T(8,128)(2,1)}), bf16[32,2,96,384]{3,2,1,0:T(8,128)(2,1)}, u32[]{:S(2)}, u32[]{:S(2)}) async-start(bf16[32,2,96,384]{3,2,1,0:T(8,128)(2,1)} %stack.22), calls=%async_computation.5 | async-start | bytes 9437184 | tf_op jit(solution)/shard_map/all_to_all | solution.py:18
  705.6 21.7 %all-to-all-start.3 = ((bf16[8,2,96,384]{3,2,1,0:T(8,128)(2,1)}), bf16[8,2,96,384]{3,2,1,0:T(8,128)(2,1)S(1)}, u32[]{:S(2)}, u32[]{:S(2)}) async-start(bf16[8,2,96,384]{3,2,1,0:T(8,128)(2,1)} %broadcast_in_dim.9), calls=%async_computation.6 | async-start | bytes 2359296 | tf_op jit(solution)/shard_map/all_to_all | solution.py:23
  730.2 112.7 %all-to-all-start.5 = ((bf16[32,2,96,384]{3,2,1,0:T(8,128)(2,1)}), bf16[32,2,96,384]{3,2,1,0:T(8,128)(2,1)}, u32[]{:S(2)}, u32[]{:S(2)}) async-start(bf16[32,2,96,384]{3,2,1,0:T(8,128)(2,1)} %stack.24), calls=%async_computation.8 | async-start | bytes 9437184 | tf_op jit(solution)/shard_map/all_to_all | solution.py:18
  848.2 14.0 %all-to-all-start.6 = ((bf16[8,1,96,384]{3,2,1,0:T(8,128)(2,1)}), bf16[8,1,96,384]{3,2,1,0:T(8,128)(2,1)S(1)}, u32[]{:S(2)}, u32[]{:S(2)}) async-start(bf16[8,1,96,384]{3,2,1,0:T(8,128)(2,1)} %broadcast_in_dim.10), calls=%async_computation.9 | async-start | bytes 1179648 | tf_op jit(solution)/shard_map/all_to_all | solution.py:23
  863.9 61.9 %all-to-all-start.7 = ((bf16[32,1,96,384]{3,2,1,0:T(8,128)(2,1)}), bf16[32,1,96,384]{3,2,1,0:T(8,128)(2,1)S(1)}, u32[]{:S(2)}, u32[]{:S(2)}) async-start(bf16[32,1,96,384]{3,2,1,0:T(8,128)(2,1)} %stack.25), calls=%async_computation.10 | async-start | bytes 4718592 | tf_op jit(solution)/shard_map/all_to_all | solution.py:18
  943.9 60.6 %all-to-all-start.9 = ((bf16[32,1,96,384]{3,2,1,0:T(8,128)(2,1)}), bf16[32,1,96,384]{3,2,1,0:T(8,128)(2,1)S(1)}, u32[]{:S(2)}, u32[]{:S(2)}) async-start(bf16[32,1,96,384]{3,2,1,0:T(8,128)(2,1)} %stack.26), calls=%async_computation.12 | async-start | bytes 4718592 | tf_op jit(solution)/shard_map/all_to_all | solution.py:18
Sparse Core Ops, SparseCore 0:
  9.8 103.6 all-gather.1
  152.7 30.9 reduce-scatter.3
  186.3 83.8 reduce-scatter.5
  272.5 22.0 reduce-scatter.7
